TPU v7x, 32 devices: a whole 2x2x4 slice. The times are simulated.
32 devices in a mesh: row: 4 (over y, core), col: 8 (over z, x).
Axes of the slice: x: 2, y: 2, z: 4, core: 2. Of those that a mesh axis runs over, the one named last changes fastest.
Arguments:
- front: float32 [12288, 12288], P('row', 'col'), may hold values from -6 to 6
- delayed: float32 [64, 12288], P('col', 'row'), may hold values from -6 to 6
- dest: int32 [64], P('col'), may hold values from 0 to 1023, as said below
- pivots: int32 [1024], replicated, may hold values from 0 to 12287, as said below
- pair_flags: int32 [1024], replicated, may hold values from 0 to 1, as said below
- linv: float32 [4, 256, 256], replicated, as said below
- dinv_diag: float32 [1024], replicated, may hold values from -0.1 to 0.1
- dinv_off: float32 [1024], replicated, may hold values from -0.08 to 0.08
Outputs:
- trailing: float32 [12288, 12288], P('row', 'col')
- factor: float32 [12288, 1024], P('row')
Inputs may be any that keep to these rules, and one draw needn't show every extreme that they name: Distinct front columns; slots p * 256 to (p + 1) * 256 - 1 are panel p's pivots. Each block of 1536 columns held by one index of col contains exactly 128 of them. `pair_flags`: A 1 at slot s joins slots s and s + 1 into one 2x2 block; no two 1s are adjacent and the last slot of a panel holds 0. `dest`: several delayed columns may share a slot. Of the 8 delayed columns held by one index of col, at most 2 go to pivot columns held by the same index of col. `linv`: each panel's matrix is unit lower triangular: ones on the diagonal, zeros above it.
All inputs are finite; a program needn't handle non-finite values.
Results may differ from a plain program's by a relative error of at most 0.00015.
Values sent between devices are 32-bit elements; how exact they have to be, the bound alone decides.
A program may use at most 192 MiB of HBM per device.

v0:
```python
import jax
import jax.numpy as jnp
from jax import lax
from jax.sharding import PartitionSpec as P

CAP = 2


precise = lax.Precision.HIGHEST


def broadcast(block, axis, holder):
    block = jnp.where(lax.axis_index(axis) == holder, block, jnp.zeros_like(block))
    return lax.psum(block, axis)


def pair_scale(scaled, pair_bits, diag_part, off_part):
    coupled = pair_bits.astype(jnp.float32) * off_part
    zero_col = jnp.zeros_like(scaled[:, :1])
    shifted_next = jnp.concatenate([scaled[:, 1:], zero_col], axis=1)
    shifted_prev = jnp.concatenate([zero_col, scaled[:, :-1]], axis=1)
    coupled_prev = jnp.concatenate([jnp.zeros_like(coupled[:1]), coupled[:-1]])
    return scaled * diag_part + shifted_next * coupled + shifted_prev * coupled_prev


def select_columns(matrix, wanted, anchor):
    block_width = matrix.shape[1]
    relative = wanted - anchor
    inside = (relative >= 0) & (relative < block_width)
    clipped = jnp.clip(relative, 0, block_width - 1)
    return jnp.where(inside[None, :], jnp.take(matrix, clipped, axis=1), 0.0)


def select_rows(matrix, wanted, anchor):
    block_height = matrix.shape[0]
    relative = wanted - anchor
    inside = (relative >= 0) & (relative < block_height)
    clipped = jnp.clip(relative, 0, block_height - 1)
    return jnp.where(inside[:, None], jnp.take(matrix, clipped, axis=0), 0.0)


def body(front, delayed, dest, pivots, pair_flags, linv, dinv_diag, dinv_off):
    col_count = lax.axis_size("col")
    rows_blk, cols_blk = front.shape
    row_start = lax.axis_index("row") * rows_blk
    col_start = lax.axis_index("col") * cols_blk
    panel_count = linv.shape[0]
    panel_width = linv.shape[1]
    slot_total = pivots.shape[0]
    slot_ids = jnp.arange(slot_total, dtype=jnp.int32)
    owner_ids = jnp.arange(col_count, dtype=jnp.int32)
    slot_hit = dest[:, None] == slot_ids[None, :]
    targets = jnp.sum(jnp.where(slot_hit, pivots[None, :], 0), axis=1)
    owners = targets // cols_blk
    within = targets - owners * cols_blk
    owner_hit = (owners[:, None] == owner_ids[None, :]).astype(jnp.int32)
    earlier = jnp.cumsum(owner_hit, axis=0) - owner_hit
    rank_in = jnp.sum(earlier * owner_hit, axis=1)
    slot_pos = jnp.arange(CAP, dtype=jnp.int32)
    placed = (owner_hit[:, :, None] > 0) & (rank_in[:, None, None] == slot_pos[None, None, :])
    send_vals = jnp.einsum("kos,kr->osr", placed.astype(jnp.float32), delayed, precision=precise)
    send_cols = jnp.sum(jnp.where(placed, within[:, None, None] + 1, 0), axis=0) - 1
    recv_vals, recv_cols = (
        lax.all_to_all(send_vals, "col", split_axis=0, concat_axis=0, tiled=True),
        lax.all_to_all(send_cols, "col", split_axis=0, concat_axis=0, tiled=True),
    )
    flat_vals = recv_vals.reshape(-1, rows_blk)
    flat_cols = recv_cols.reshape(-1)
    col_ids = jnp.arange(cols_blk, dtype=jnp.int32)
    col_hit = (flat_cols[:, None] == col_ids[None, :]).astype(jnp.float32)
    current = front + lax.dot_general(
        flat_vals, col_hit, (((0,), (0,)), ((), ())), precision=precise
    )
    factors = []
    piv_owner = pivots // cols_blk
    piv_hit = (piv_owner[:, None] == owner_ids[None, :]).astype(jnp.int32)
    piv_rank = jnp.sum((jnp.cumsum(piv_hit, axis=0) - piv_hit) * piv_hit, axis=1)
    per_owner = slot_total // col_count
    owned_here = piv_owner == lax.axis_index("col")
    rank_ids = jnp.arange(per_owner, dtype=jnp.int32)
    own_slots = jnp.sum(
        jnp.where(
            owned_here[None, :] & (piv_rank[None, :] == rank_ids[:, None]), slot_ids[None, :], 0
        ),
        axis=1,
    )
    compact = select_columns(current, pivots[own_slots], col_start)
    gathered = lax.all_gather(compact, "col", axis=1, tiled=True)
    every_panel = jnp.take(gathered, piv_owner * per_owner + piv_rank, axis=1)
    previous = []
    for panel_index in range(panel_count):
        offset = panel_index * panel_width
        panel_cols = every_panel[:, offset : offset + panel_width]
        for cols_before, rows_before in previous:
            panel_cols = panel_cols - lax.dot_general(
                cols_before,
                rows_before[offset : offset + panel_width],
                (((1,), (1,)), ((), ())),
                precision=precise,
            )
        finish_offset = panel_index * panel_width
        finish_scaled = jnp.dot(panel_cols, jnp.transpose(linv[panel_index]), precision=precise)
        finish_columns = pair_scale(
            finish_scaled,
            pair_flags[finish_offset : finish_offset + panel_width],
            dinv_diag[finish_offset : finish_offset + panel_width],
            dinv_off[finish_offset : finish_offset + panel_width],
        )
        root_row = col_start // rows_blk
        slice_start = jnp.clip(col_start - row_start, 0, rows_blk - cols_blk)
        root_piece = lax.dynamic_slice_in_dim(finish_scaled, slice_start, cols_blk, 0)
        col_scaled = broadcast(root_piece, "row", root_row)
        current = current - lax.dot_general(
            finish_columns, col_scaled, (((1,), (1,)), ((), ())), precision=precise
        )
        factors.append(finish_columns)
        if panel_index + 1 < panel_count:
            pivot_part = select_rows(finish_scaled, pivots, row_start)
            pivot_rows = lax.psum(pivot_part, "row")
            previous.append((finish_columns, pivot_rows))
    row_ids = row_start + jnp.arange(rows_blk, dtype=jnp.int32)
    row_in = jnp.any(row_ids[:, None] == pivots[None, :], axis=1)
    col_in = jnp.any((col_start + col_ids)[:, None] == pivots[None, :], axis=1)
    trailing = jnp.where(row_in[:, None] | col_in[None, :], 0.0, current)
    factor = jnp.concatenate(factors, axis=1)
    return (trailing, factor)


def solution(mesh):
    return jax.shard_map(
        body,
        mesh=mesh,
        in_specs=(P("row", "col"), P("col", "row"), P("col"), P(), P(), P(), P(), P()),
        out_specs=(P("row", "col"), P("row", None)),
        check_vma=False,
    )
```

profile of v0, /device:TPU:5, one launch (start us, length us, event | category | flops | bytes accessed | tf_op | source)
XLA Modules:
  0.0 719.3 jit_solution(9475887452106300543)
XLA Ops:
  9.2 5.5 all-to-all-start.1
  16.5 2.3 reduce-window.6
  21.1 5.4 all-to-all-start
  27.9 5.3 all-to-all-done
  33.3 18.0 %convolution_add_fusion = f32[3072,1536]{1,0:T(8,128)} fusion(f32[3072,1536]{1,0:T(8,128)} %param.10, f32[16,3072]{1,0:T(8,128)S(1)} %reshape.189, s32[16]{0:T(128)S(1)} %eq.152), kind=kOutput, calls=%fused_computation.7 | convolution fusion | flops 910712832 | bytes 37945408 | tf_op jit(solution)/shard_map/dot_general | solution.py:71
  51.3 18.7 %copy.33 = f32[3072,1536]{0,1:T(8,128)} copy(f32[3072,1536]{1,0:T(8,128)} %convolution_add_fusion) | data formatting | bytes 37748736 | tf_op jit(solution)/shard_map/add | solution.py:71
  70.0 8.2 %gather_fusion.1 = f32[128,3072]{1,0:T(8,128)S(1)} fusion(f32[3072,1536]{0,1:T(8,128)} %copy.33, s32[1024]{0:T(1024)S(1)} %pad_clamp_fusion), kind=kCustom, calls=%fused_computation.4 | custom fusion | bytes 3146240 | tf_op jit(solution)/shard_map/jit(_take)/gather | solution.py:31
  80.4 175.0 %all-gather.2.cloned.1.call-done = f32[3072,1024]{0,1:T(8,128)} async-done(((f32[3072,128]{0,1:T(8,128)}), f32[3072,1024]{0,1:T(8,128)}) %all-gather.2.cloned.1.call-update) | async-done | bytes 12582928 | tf_op jit(solution)/shard_map/all_gather | solution.py:88
  255.4 16.5 %gather_fusion.2 = f32[1024,3072]{1,0:T(8,128)} fusion(f32[3072,1024]{0,1:T(8,128)} %all-gather.2.cloned.1.call-done, s32[1024]{0:T(1024)S(1)} %broadcast_clamp_fusion), kind=kCustom, calls=%fused_computation.5 | custom fusion | bytes 25169920 | tf_op jit(solution)/shard_map/jit(_take)/gather | solution.py:89
  271.9 12.6 %copy.34 = f32[1024,3072]{0,1:T(8,128)} copy(f32[1024,3072]{1,0:T(8,128)} %gather_fusion.2) | data formatting | bytes 25165824 | tf_op jit(solution)/shard_map/jit(_take)/gather | solution.py:89
  284.5 12.4 %select_bitcast_fusion = f32[3072,1024]{1,0:T(8,128)} fusion(f32[1024,3072]{0,1:T(8,128)} %copy.34, pred[1024]{0:T(1024)(128)(4,1)S(1)} %compare_and_fusion.2), kind=kLoop, calls=%fused_computation.9 | loop fusion | flops 3145728 | bytes 25166848 | tf_op jit(solution)/shard_map/jit(_take)/select_n | solution.py:89
  296.9 4.8 fusion
  301.7 3.7 fusion.40
  305.4 2.3 copy.35
  307.8 5.3 gather_fusion.3
  315.1 5.2 multiply_add_fusion.3
  321.9 27.2 %all-reduce.14.cloned.1.call-done = f32[1024,256]{1,0:T(8,128)} async-done(((f32[1024,256]{1,0:T(8,128)}), f32[1024,256]{1,0:T(8,128)}) %all-reduce.14.cloned.1.call-update) | async-done | bytes 1048592 | tf_op jit(solution)/shard_map/psum | solution.py:119
  349.2 7.3 %convolution_subtract_fusion.5 = f32[3072,256]{1,0:T(8,128)S(1)} fusion(f32[3072,256]{0,1:T(8,128)S(1)} %multiply_add_fusion.3, f32[3072,1024]{1,0:T(8,128)} %select_bitcast_fusion, f32[1024,256]{1,0:T(8,128)} %all-reduce.14.cloned.1.call-done), kind=kOutput, calls=%fused_computation.17 | convolution fusion | flops 2416705536 | bytes 9699328 | tf_op jit(solution)/shard_map/dot_general | solution.py:95
  356.5 4.1 fusion.13
  362.3 3.3 fusion.39
  365.6 3.5 copy.36
  369.1 6.6 gather_fusion.4
  375.7 2.5 select_select_fusion.1
  378.5 7.0 multiply_add_fusion.2
  385.4 8.0 %convolution_subtract_fusion.4 = f32[3072,256]{1,0:T(8,128)} fusion(f32[3072,256]{0,1:T(8,128)S(1)} %multiply_add_fusion.3, f32[3072,1024]{1,0:T(8,128)} %select_bitcast_fusion, f32[1024,256]{1,0:T(8,128)S(1)} %copy-done.19), kind=kOutput, calls=%fused_computation.16 | convolution fusion | flops 2416705536 | bytes 9699328 | tf_op jit(solution)/shard_map/dot_general | solution.py:95
  395.1 8.1 %convolution_subtract_fusion.2 = f32[3072,256]{1,0:T(8,128)} fusion(f32[3072,256]{0,1:T(8,128)S(1)} %multiply_add_fusion.3, f32[3072,1024]{1,0:T(8,128)} %select_bitcast_fusion, f32[1024,256]{1,0:T(8,128)S(1)} %copy-done.19), kind=kOutput, calls=%fused_computation.14 | convolution fusion | flops 2416705536 | bytes 9699328 | tf_op jit(solution)/shard_map/dot_general | solution.py:95
  403.2 12.0 %all-reduce.16.cloned.1.call-done = f32[1024,256]{1,0:T(8,128)} async-done(((f32[1024,256]{1,0:T(8,128)}), f32[1024,256]{1,0:T(8,128)}) %all-reduce.16.cloned.1.call-update) | async-done | bytes 1048592 | tf_op jit(solution)/shard_map/psum | solution.py:119
  415.1 8.3 %convolution_subtract_fusion.3 = f32[3072,256]{1,0:T(8,128)S(1)} fusion(f32[3072,256]{1,0:T(8,128)} %convolution_subtract_fusion.4, f32[3072,256]{0,1:T(8,128)} %multiply_add_fusion.2, f32[1024,256]{1,0:T(8,128)} %all-reduce.16.cloned.1.call-done), kind=kOutput, calls=%fused_computation.15 | convolution fusion | flops 2416705536 | bytes 9699328 | tf_op jit(solution)/shard_map/dot_general | solution.py:95
  423.5 4.1 fusion.11
  427.6 1.7 copy-done.2
  429.3 3.3 fusion.38
  432.5 3.5 copy.37
  436.1 6.6 gather_fusion.5
  442.7 2.6 select_select_fusion
  445.8 7.0 multiply_add_fusion.1
  455.3 8.1 %convolution_subtract_fusion.1 = f32[3072,256]{1,0:T(8,128)} fusion(f32[3072,256]{1,0:T(8,128)S(1)} %copy-done.16, f32[3072,256]{0,1:T(8,128)S(1)} %copy-done.8, f32[1024,256]{1,0:T(8,128)} %all-reduce.16.cloned.1.call-done), kind=kOutput, calls=%fused_computation.13 | convolution fusion | flops 2416705536 | bytes 9699328 | tf_op jit(solution)/shard_map/dot_general | solution.py:95
  463.4 18.8 %all-reduce.18.cloned.1.call-done = f32[1024,256]{1,0:T(8,128)} async-done(((f32[1024,256]{1,0:T(8,128)}), f32[1024,256]{1,0:T(8,128)}) %all-reduce.18.cloned.1.call-update) | async-done | bytes 1048592 | tf_op jit(solution)/shard_map/psum | solution.py:119
  482.2 8.3 %convolution_subtract_fusion = f32[3072,256]{1,0:T(8,128)S(1)} fusion(f32[3072,256]{1,0:T(8,128)} %convolution_subtract_fusion.1, f32[3072,256]{0,1:T(8,128)} %multiply_add_fusion.1, f32[1024,256]{1,0:T(8,128)} %all-reduce.18.cloned.1.call-done), kind=kOutput, calls=%fused_computation.12 | convolution fusion | flops 2416705536 | bytes 9699328 | tf_op jit(solution)/shard_map/dot_general | solution.py:95
  490.5 4.2 fusion.9
  499.2 2.0 compare_reduce_fusion
  501.2 3.8 fusion.37
  509.7 5.4 pad_maximum_fusion
  515.1 12.7 %copy.38 = f32[3072,1024]{1,0:T(8,128)} copy(f32[3072,1024]{0,1:T(8,128)} %pad_maximum_fusion) | data formatting | bytes 25165824
  527.8 90.5 %all-reduce.20.cloned.1.call-done = (f32[1536,256]{0,1:T(8,128)}, f32[1536,256]{0,1:T(8,128)}, f32[1536,256]{0,1:T(8,128)}, f32[1536,256]{0,1:T(8,128)}) async-done(((f32[1536,256]{0,1:T(8,128)}, f32[1536,256]{0,1:T(8,128)}, f32[1536,256]{0,1:T(8,128)}, f32[1536,256]{0,1:T(8,128)}), (f32[1536,256]{0,1:T(8,128)}, f32[1536,256]{0,1:T(8,128)}, f32[1536,256]{0,1:T(8,128)}, ...) | async-done | bytes 6291472 | tf_op jit(solution)/shard_map/psum | solution.py:14
  618.3 19.9 %fusion.44 = f32[3072,1536]{1,0:T(8,128)} fusion(f32[3072,256]{0,1:T(8,128)} %multiply_add_fusion.1, f32[1536,256]{0,1:T(8,128)} %get-tuple-element.11), kind=kOutput, calls=%fused_computation.119 | convolution fusion | flops 14495514624 | bytes 23592960 | tf_op jit(solution)/shard_map/dot_general | solution.py:113
  638.2 18.3 %fusion.43 = f32[3072,1536]{1,0:T(8,128)} fusion(f32[3072,256]{0,1:T(8,128)S(1)} %copy-done.10, f32[1536,256]{0,1:T(8,128)S(1)} %copy-done.18), kind=kOutput, calls=%fused_computation.118 | convolution fusion | flops 14495514624 | bytes 23592960 | tf_op jit(solution)/shard_map/dot_general | solution.py:113
  656.4 17.9 %fusion.42 = f32[3072,1536]{1,0:T(8,128)} fusion(f32[3072,256]{0,1:T(8,128)S(1)} %multiply_add_fusion.3, f32[1536,256]{0,1:T(8,128)S(1)} %copy-done.17), kind=kOutput, calls=%fused_computation.117 | convolution fusion | flops 14495514624 | bytes 23592960 | tf_op jit(solution)/shard_map/dot_general | solution.py:113
  674.4 38.1 %subtract_select_fusion = f32[3072,1536]{1,0:T(8,128)} fusion(f32[3072,1536]{1,0:T(8,128)} %fusion.44, f32[3072,1536]{1,0:T(8,128)} %fusion.43, f32[3072,1536]{1,0:T(8,128)} %convolution_add_fusion, f32[3072,1536]{1,0:T(8,128)} %fusion.42, f32[3072,256]{0,1:T(8,128)} %copy-done.15, f32[1536,256]{0,1:T(8,128)} %get-tuple-element.14, ...), kind=kOutput, calls=%fused_computation.6 | convolution fusion | flops 14523826176 | bytes 99095040 | tf_op jit(solution)/shard_map/dot_general | solution.py:113
  (102 shorter events, 28.6 us)
Async XLA Ops:
  7.2 7.5 %copy-start = (f32[8,3072]{1,0:T(8,128)S(1)}, f32[8,3072]{1,0:T(8,128)}, u32[]{:S(2)}) copy-start(f32[8,3072]{1,0:T(8,128)} %param.11) | copy-start | bytes 294916
  9.2 12.0 %all-to-all-start.1 = ((s32[8,1,2]{2,1,0:T(1,128)}), s32[8,1,2]{2,1,0:T(1,128)S(1)}, u32[]{:S(2)}, u32[]{:S(2)}) async-start(s32[8,1,2]{2,1,0:T(1,128)} %copy.32), calls=%async_computation.1 | async-start | bytes 8192 | tf_op jit(solution)/shard_map/all_to_all | solution.py:65
  21.1 12.1 %all-to-all-start = ((f32[8,2,3072]{2,1,0:T(2,128)}), f32[8,2,3072]{2,1,0:T(2,128)S(1)}, u32[]{:S(2)}, u32[]{:S(2)}) async-start(f32[8,2,3072]{2,1,0:T(2,128)} %copy.31), calls=%async_computation | async-start | bytes 393216 | tf_op jit(solution)/shard_map/all_to_all | solution.py:64
  26.6 228.8 %all-gather.2.cloned.1.call-start = ((), (), s32[]{:S(2)}) async-start(), calls=%async_computation.2 | async-start | bytes 14155776 | tf_op jit(solution)/shard_map/all_gather | solution.py:88
  78.2 1.9 copy-start.20
  78.2 1.9 copy-start.21
  78.2 2.0 copy-start.11
  78.2 2.0 copy-start.22
  79.7 269.5 %all-reduce.14.cloned.1.call-start = ((), (), s32[]{:S(2)}) async-start(), calls=%async_computation.3 | async-start | bytes 2097152 | tf_op jit(solution)/shard_map/psum | solution.py:119
  301.7 3.7 copy-start.6
  314.5 100.7 %all-reduce.16.cloned.1.call-start = ((), (), s32[]{:S(2)}) async-start(), calls=%async_computation.4 | async-start | bytes 2097152 | tf_op jit(solution)/shard_map/psum | solution.py:119
  315.1 5.2 copy-start.7
  360.6 1.7 copy-start.4
  378.2 103.9 %all-reduce.18.cloned.1.call-start = ((), (), s32[]{:S(2)}) async-start(), calls=%async_computation.5 | async-start | bytes 2097152 | tf_op jit(solution)/shard_map/psum | solution.py:119
  378.5 7.0 copy-start.19
  385.4 8.0 %copy-start.5 = (f32[3072,256]{0,1:T(8,128)S(1)}, f32[3072,256]{0,1:T(8,128)}, u32[]{:S(2)}) copy-start(f32[3072,256]{0,1:T(8,128)} %copy-done.4) | copy-start | bytes 9437188
  427.6 1.7 copy-start.2
  445.3 173.0 %all-reduce.20.cloned.1.call-start = ((), (), s32[]{:S(2)}) async-start(), calls=%async_computation.6 | async-start | bytes 12582912 | tf_op jit(solution)/shard_map/psum | solution.py:14
  445.7 7.1 copy-start.3
  445.8 8.7 %copy-start.16 = (f32[3072,256]{1,0:T(8,128)S(1)}, f32[3072,256]{1,0:T(8,128)}, u32[]{:S(2)}) copy-start(f32[3072,256]{1,0:T(8,128)} %convolution_subtract_fusion.2) | copy-start | bytes 9437188
  452.8 2.5 copy-start.8
  494.8 1.7 copy-start.12
  501.2 3.9 copy-start.13
  505.1 3.0 copy-start.9
  505.1 4.6 copy-start.14
  506.4 1.7 copy-start.15
  618.3 19.9 %copy-start.10 = (f32[3072,256]{0,1:T(8,128)S(1)}, f32[3072,256]{0,1:T(8,128)}, u32[]{:S(2)}) copy-start(f32[3072,256]{0,1:T(8,128)} %multiply_add_fusion.2) | copy-start | bytes 9437188
  618.3 19.9 %copy-start.18 = (f32[1536,256]{0,1:T(8,128)S(1)}, f32[1536,256]{0,1:T(8,128)}, u32[]{:S(2)}) copy-start(f32[1536,256]{0,1:T(8,128)} %get-tuple-element.12) | copy-start | bytes 4718596
  638.2 18.3 %copy-start.17 = (f32[1536,256]{0,1:T(8,128)S(1)}, f32[1536,256]{0,1:T(8,128)}, u32[]{:S(2)}) copy-start(f32[1536,256]{0,1:T(8,128)} %get-tuple-element.13) | copy-start | bytes 4718596
  674.4 38.1 %copy-start.1 = (f32[8,3072]{1,0:T(8,128)S(1)}, f32[8,3072]{1,0:T(8,128)}, u32[]{:S(2)}) copy-start(f32[8,3072]{1,0:T(8,128)} %param.11) | copy-start | bytes 294916
Sparse Core Ops, SparseCore 0:
  79.8 175.5 all-gather.1
  314.6 34.5 all-reduce.13
  378.4 36.7 all-reduce.15
  445.4 36.7 all-reduce.17
  498.3 119.9 all-reduce.19
where the time goes:
time: 728 us; the launch traced here: 719 us
  waiting for transfers between devices  329 us (45%)
  matrix products  178 us (24%)
  local copies, waits for them, and re-layouts  124 us (17%)
  other arithmetic  61.5 us (8%)
  between operations  14.5 us (2%)
  starting transfers between devices  12.6 us (2%)
    all_gather x1, waiting for transfers between devices, body(): gathered = lax.all_gather(compact, 'col', axis=1, tiled=True)  175 us
    dot_general x4, matrix products, body(): lax.dot_general(finish_columns, col_scaled, (((1,), (1,)), ((), ())), pre...  94.2 us
    psum x1, waiting for transfers between devices, broadcast(): return lax.psum(block, axis)  90.5 us
    psum x3, waiting for transfers between devices, body(): pivot_rows = lax.psum(pivot_part, 'row')  58 us
    dot_general x6, matrix products, body(): lax.dot_general(cols_before, rows_before[offset:offset + panel_width], ((...  48.2 us
    gather x2, local copies, waits for them, and re-layouts, body(): every_panel = jnp.take(gathered, piv_owner * per_owner + piv_rank, axis=1)  29.1 us
    unnamed x47, local copies, waits for them, and re-layouts  21.9 us
    add x4, other arithmetic, pair_scale(): scaled * diag_part + shifted_next * coupled + shifted_prev * coupled_prev  20.5 us
  transfers between devices with their start and end apart: 7, of which 6 were waited for; matrix products, arithmetic and copies ran while one was open for 11% of the time, Pallas kernels for 0%

commit v1 on v0

v1 whole, which is shorter than its diff:
```python
import functools

import jax
import jax.numpy as jnp
from jax import lax
from jax.experimental import pallas as pl
from jax.experimental.pallas import tpu as pltpu
from jax.sharding import PartitionSpec as P

MESH = pl.DeviceIdType.MESH
VMEM_LIMIT = 60 * 1024 * 1024


def dot(a, b, ca, cb):
    return lax.dot_general(a, b, (((ca,), (cb,)), ((), ())), precision=lax.Precision.HIGHEST)


def pick(ones, a, c1, ca):
    total = None
    for _ in range(3):
        part = lax.reduce_precision(a, 8, 7)
        a = a - part
        term = lax.dot_general(
            ones.astype(jnp.bfloat16), part.astype(jnp.bfloat16), (((c1,), (ca,)), ((), ())),
            preferred_element_type=jnp.float32,
        )
        total = term if total is None else total + term
    return total


def onehot(a, b):
    return (a[:, None] == b[None, :]).astype(jnp.float32)


def pair_scale(scaled, panel_width, pair_flags, diag_part, off_part):
    total = scaled.shape[1]
    slot = lax.broadcasted_iota(jnp.int32, (total,), 0) % panel_width
    coupled = pair_flags.astype(jnp.float32) * off_part
    up = jnp.where(slot == panel_width - 1, 0.0, coupled)
    down = jnp.where(slot == 0, 0.0, jnp.roll(coupled, 1))
    nxt = jnp.roll(scaled, -1, axis=1)
    prv = jnp.roll(scaled, 1, axis=1)
    return scaled * diag_part + nxt * up + prv * down


def gather_kernel(zs, xs, ys, halves, own_ref, all_ref, col_ref, copy_sem, root_sem, all_send, all_recv, col_send, col_recv):
    row, col = lax.axis_index("row"), lax.axis_index("col")
    y, k = row // 2, row % 2
    z, x = col // xs, col % xs
    root = col // halves
    half = col % halves
    root_y, root_k = root // 2, root % 2
    is_root = row == root
    at_root_core = k == root_k

    def at(y_, k_, z_, x_):
        return (y_ * 2 + k_, z_ * xs + x_)

    links = [
        (z + 1 < zs, at(y, k, z + 1, x)),
        (z >= 1, at(y, k, z - 1, x)),
        (x + 1 < xs, at(y, k, z, x + 1)),
        (x >= 1, at(y, k, z, x - 1)),
        (y + 1 < ys, at(y + 1, k, z, x)),
        (y >= 1, at(y - 1, k, z, x)),
        (True, at(y, 1 - k, z, x)),
    ]

    def when(cond, fn):
        if cond is True:
            fn()
        else:
            pl.when(cond)(fn)

    barrier = pltpu.get_barrier_semaphore()
    for cond, dev in links:
        when(cond, lambda dev=dev: pl.semaphore_signal(barrier, inc=1, device_id=dev, device_id_type=MESH))
    peers = 1
    for cond, _ in links[:6]:
        peers = peers + jnp.where(cond, 1, 0)
    pl.semaphore_wait(barrier, peers)

    def block(b, c):
        return all_ref.at[b, c]

    def send_all(way, b, c, src, act):
        act(pltpu.make_async_remote_copy(
            src_ref=src, dst_ref=block(b, c), send_sem=all_send.at[way, b, c], recv_sem=all_recv.at[b, c],
            device_id=links[way][1], device_id_type=MESH))

    def send_col(way, c, src, act):
        act(pltpu.make_async_remote_copy(
            src_ref=src, dst_ref=col_ref.at[c], send_sem=col_send.at[way, c], recv_sem=col_recv.at[c],
            device_id=links[4 + way][1], device_id_type=MESH))

    def arrived(b, c):
        pltpu.make_async_copy(block(b, c), block(b, c), all_recv.at[b, c]).wait()

    def spread_col(c, src, up, down, act):
        when((y + 1 < ys) & up, lambda: send_col(0, c, src, act))
        when((y >= 1) & down, lambda: send_col(1, c, src, act))
        send_col(2, c, src, act)

    def on_block(c, mine, act, draining):
        def go():
            src = own_ref.at[half] if mine else block(half, c)
            spread_col(c, src, True, True, act)
            local = pltpu.make_async_copy(src, col_ref.at[c], root_sem.at[c])
            if draining:
                local.wait()
            else:
                local.start()
        when(is_root, go)

    def on_col(c, act, draining):
        def go():
            if not draining:
                pltpu.make_async_copy(col_ref.at[c], col_ref.at[c], col_recv.at[c]).wait()
            spread_col(c, col_ref.at[c], y > root_y, y < root_y, act)
        when(at_root_core & (y != root_y), go)

    def steps(act, draining):
        pending = []

        def later(cond, c):
            pending.append((cond, c))
            if len(pending) > 3:
                flush()

        def flush():
            cond, c = pending.pop(0)
            when(cond, lambda: on_col(c, act, draining))

        for t in range(zs + xs - 1):
            if t < zs:
                for sign in ((0,) if t == 0 else (-1, 1)):
                    zc = z + sign * t
                    here = True if t == 0 else (zc >= 0) & (zc < zs)
                    c = zc * xs + x

                    def go(c=c, sign=sign, t=t):
                        for b in range(halves):
                            if t and not draining:
                                arrived(b, c)
                            src = own_ref.at[b] if t == 0 else block(b, c)
                            when(x + 1 < xs, lambda: send_all(2, b, c, src, act))
                            when(x >= 1, lambda: send_all(3, b, c, src, act))
                            if sign <= 0:
                                when(z + 1 < zs, lambda: send_all(0, b, c, src, act))
                            if sign >= 0:
                                when(z >= 1, lambda: send_all(1, b, c, src, act))
                        on_block(c, t == 0, act, draining)
                    when(here, go)
                    later(here, c)
            for d in range(1, xs):
                tz = t - d
                if tz < 0 or tz >= zs:
                    continue
                for sign in ((0,) if tz == 0 else (-1, 1)):
                    for side in (-1, 1):
                        zc, xc = z + sign * tz, x + side * d
                        here = (zc >= 0) & (zc < zs) & (xc >= 0) & (xc < xs)
                        c = zc * xs + xc

                        def go(c=c, side=side):
                            for b in range(halves):
                                if not draining:
                                    arrived(b, c)
                                if side < 0:
                                    when(x + 1 < xs, lambda: send_all(2, b, c, block(b, c), act))
                                else:
                                    when(x >= 1, lambda: send_all(3, b, c, block(b, c), act))
                            on_block(c, False, act, draining)
                        when(here, go)
                        later(here, c)
        while pending:
            flush()

    keep = [pltpu.make_async_copy(own_ref.at[b], block(b, col), copy_sem.at[b]) for b in range(halves)]
    for copy in keep:
        copy.start()
    steps(lambda copy: copy.start(), False)
    for copy in keep:
        copy.wait()
    steps(lambda copy: copy.wait_send(), True)

    def last():
        for c in range(zs * xs):
            pltpu.make_async_copy(col_ref.at[c], col_ref.at[c], col_recv.at[c]).wait()
    when(k != root_k, last)


def exchange(own, halves, height):
    n_col = lax.axis_size("col")
    n_row = lax.axis_size("row")
    slots = own.shape[1]
    ys = n_row // 2
    xs = ys if n_col % ys == 0 else 1
    zs = n_col // xs
    vmem = pl.BlockSpec(memory_space=pltpu.VMEM)
    every, cols = pl.pallas_call(
        functools.partial(gather_kernel, zs, xs, ys, halves),
        out_shape=(
            jax.ShapeDtypeStruct((halves, n_col, height, slots), jnp.float32),
            jax.ShapeDtypeStruct((n_col, height, slots), jnp.float32),
        ),
        in_specs=[vmem],
        out_specs=(vmem, vmem),
        scratch_shapes=[
            pltpu.SemaphoreType.DMA((halves,)),
            pltpu.SemaphoreType.DMA((n_col,)),
            pltpu.SemaphoreType.DMA((4, halves, n_col)),
            pltpu.SemaphoreType.DMA((halves, n_col)),
            pltpu.SemaphoreType.DMA((3, n_col)),
            pltpu.SemaphoreType.DMA((n_col,)),
        ],
        compiler_params=pltpu.CompilerParams(
            collective_id=0, has_side_effects=True, vmem_limit_bytes=VMEM_LIMIT
        ),
    )(own.reshape(halves, height, slots))
    return every.reshape(halves * n_col * height, slots), cols.reshape(n_col * height, slots)


def trailing_kernel(tile, s_ref, c_ref, front_ref, rkeep_ref, ckeep_ref, coef_ref, out_ref, factor_ref, chi, clo):
    slots = s_ref.shape[1]
    cols = c_ref.shape[0]

    @pl.when(pl.program_id(0) == 0)
    def _():
        @pl.loop(0, cols // tile)
        def _(i):
            part = pl.ds(pl.multiple_of(i * tile, tile), tile)
            block = c_ref[part, :].T
            hi = block.astype(jnp.bfloat16)
            chi[:, part] = hi
            clo[:, part] = (block - hi.astype(jnp.float32)).astype(jnp.bfloat16)

    s = s_ref[...]
    columns = (
        s * coef_ref[0:1, :]
        + pltpu.roll(s, slots - 1, 1) * coef_ref[1:2, :]
        + pltpu.roll(s, 1, 1) * coef_ref[2:3, :]
    )
    factor_ref[...] = columns
    hi = columns.astype(jnp.bfloat16)
    lo = (columns - hi.astype(jnp.float32)).astype(jnp.bfloat16)
    rkeep = rkeep_ref[...] > 0.0

    @pl.loop(0, cols // tile)
    def _(i):
        part = pl.ds(pl.multiple_of(i * tile, tile), tile)
        bh, bl = chi[:, part], clo[:, part]
        acc = jnp.dot(hi, bh, preferred_element_type=jnp.float32)
        acc += jnp.dot(hi, bl, preferred_element_type=jnp.float32)
        acc += jnp.dot(lo, bh, preferred_element_type=jnp.float32)
        out_ref[:, part] = jnp.where(rkeep & (ckeep_ref[:, part] > 0.0), front_ref[:, part] - acc, 0.0)


def update(every, col_scaled, front, row_keep, col_keep, coef):
    rows, cols = front.shape
    slots = every.shape[1]
    tile = 256
    return pl.pallas_call(
        functools.partial(trailing_kernel, tile),
        grid=(rows // tile,),
        in_specs=[
            pl.BlockSpec((tile, slots), lambda i: (i, 0)),
            pl.BlockSpec((cols, slots), lambda i: (0, 0)),
            pl.BlockSpec((tile, cols), lambda i: (i, 0)),
            pl.BlockSpec((tile, 1), lambda i: (i, 0)),
            pl.BlockSpec((1, cols), lambda i: (0, 0)),
            pl.BlockSpec((8, slots), lambda i: (0, 0)),
        ],
        out_specs=(
            pl.BlockSpec((tile, cols), lambda i: (i, 0)),
            pl.BlockSpec((tile, slots), lambda i: (i, 0)),
        ),
        out_shape=(
            jax.ShapeDtypeStruct((rows, cols), jnp.float32),
            jax.ShapeDtypeStruct((rows, slots), jnp.float32),
        ),
        scratch_shapes=[pltpu.VMEM((slots, cols), jnp.bfloat16), pltpu.VMEM((slots, cols), jnp.bfloat16)],
        compiler_params=pltpu.CompilerParams(
            dimension_semantics=("arbitrary",), vmem_limit_bytes=VMEM_LIMIT
        ),
    )(every, col_scaled, front, row_keep, col_keep, coef)


def body(front, delayed, dest, pivots, pair_flags, linv, dinv_diag, dinv_off):
    n_col = lax.axis_size("col")
    n_row = lax.axis_size("row")
    rows_blk, cols_blk = front.shape
    row_id = lax.axis_index("row")
    col_id = lax.axis_index("col")
    row_start = row_id * rows_blk
    col_start = col_id * cols_blk
    panels, width, _ = linv.shape
    slots = pivots.shape[0]
    per_col = slots // n_col
    per_row = slots // n_row
    ndel = delayed.shape[0]
    halves = rows_blk // cols_blk
    height = cols_blk // n_col
    slot_ids = jnp.arange(slots, dtype=jnp.int32)

    col_owner = pivots // cols_blk
    row_owner = pivots // rows_blk
    before = slot_ids[None, :] < slot_ids[:, None]
    col_rank = jnp.sum((before & (col_owner[:, None] == col_owner[None, :])).astype(jnp.int32), axis=1)
    row_rank = jnp.sum((before & (row_owner[:, None] == row_owner[None, :])).astype(jnp.int32), axis=1)
    col_rel = jnp.where(col_owner == col_id, pivots - col_start, -1)
    row_rel = jnp.where(row_owner == row_id, pivots - row_start, -1)
    col_want = jnp.sum(
        jnp.where((col_owner == col_id)[None, :] & (col_rank[None, :] == jnp.arange(per_col)[:, None]), col_rel[None, :], 0),
        axis=1,
    )
    row_want = jnp.sum(
        jnp.where((row_owner == row_id)[None, :] & (row_rank[None, :] == jnp.arange(per_row)[:, None]), row_rel[None, :], 0),
        axis=1,
    )

    picked = pick(onehot(col_want, jnp.arange(cols_blk)), front, 1, 1)
    mine = jnp.concatenate([picked, delayed], axis=0)
    wide = per_col + ndel

    piv_part = pick(onehot(row_want, jnp.arange(rows_blk)), mine, 1, 1).T
    slot_row = jnp.pad(dest.astype(jnp.float32)[None, :], ((0, 7), (0, per_row - ndel)))
    piv_all = lax.all_gather(jnp.concatenate([piv_part, slot_row], axis=0), ("row", "col"), axis=0, tiled=False)
    piv_all = piv_all.reshape(n_row, n_col, wide + 8, per_row)
    dest_all = piv_all[0, :, wide, :ndel].astype(jnp.int32)
    piv_all = piv_all[:, :, :wide].reshape(n_row, n_col * wide, per_row)
    share = mine.reshape(wide, halves, n_col, height).transpose(2, 0, 1, 3)
    share = share.reshape(n_col, wide, halves * height)
    share = lax.all_to_all(share, "col", split_axis=0, concat_axis=0, tiled=True)
    share = share.reshape(n_col * wide, halves * height)

    home = jnp.where(
        jnp.arange(wide)[None, :] < per_col,
        jnp.arange(n_col)[:, None] * per_col + jnp.arange(wide)[None, :],
        -1,
    )
    is_col = home.reshape(-1)[:, None] == (col_owner * per_col + col_rank)[None, :]
    dest_wide = jnp.concatenate([jnp.full((n_col, per_col), -1, jnp.int32), dest_all], axis=1)
    is_del = dest_wide.reshape(-1)[:, None] == slot_ids[None, :]
    take = (is_col | is_del).astype(jnp.float32)
    stacked = jnp.concatenate([piv_all[r] for r in range(n_row)] + [share], axis=1)
    current = dot(stacked, take, 0, 0)
    to_slot = onehot(row_owner * per_row + row_rank, slot_ids)

    done = []
    parts = []
    for p in range(panels):
        lo, hi = p * width, (p + 1) * width
        cols = current[:, lo:hi]
        for earlier_cols, earlier_rows, start in done:
            cols = cols - dot(earlier_cols, earlier_rows[lo - start : hi - start], 1, 1)
        scaled = dot(cols, linv[p], 1, 1)
        parts.append(scaled[slots:])
        if p + 1 < panels:
            columns = pair_scale(scaled, width, pair_flags[lo:hi], dinv_diag[lo:hi], dinv_off[lo:hi])
            rows = pick(to_slot[hi:], scaled[:slots], 1, 0)
            done.append((columns, rows, hi))
    own = jnp.concatenate(parts, axis=1)

    every, col_scaled = exchange(own, halves, height)
    in_panel = slot_ids % width
    coupled = pair_flags.astype(jnp.float32) * dinv_off
    zero = jnp.zeros_like(dinv_diag)
    coef = jnp.stack(
        [dinv_diag, jnp.where(in_panel == width - 1, 0.0, coupled), jnp.where(in_panel == 0, 0.0, jnp.roll(coupled, 1))]
        + [zero] * 5
    )
    row_in = jnp.any((row_start + jnp.arange(rows_blk))[:, None] == pivots[None, :], axis=1)
    col_in = jnp.any((col_start + jnp.arange(cols_blk))[:, None] == pivots[None, :], axis=1)
    row_keep = jnp.where(row_in, 0.0, 1.0)[:, None]
    col_keep = jnp.where(col_in, 0.0, 1.0)[None, :]
    trailing, factor = update(every, col_scaled, front, row_keep, col_keep, coef)
    return (trailing, factor)


def solution(mesh):
    return jax.shard_map(
        body,
        mesh=mesh,
        in_specs=(P("row", "col"), P("col", "row"), P("col"), P(), P(), P(), P(), P()),
        out_specs=(P("row", "col"), P("row", None)),
        check_vma=False,
    )
```

time: 728 us -> 423 us (0.58)
  waiting for transfers between devices: 329 us -> 53.4 us
  Pallas kernels: 0 us -> 220 us
  matrix products: 178 us -> 77.9 us
  local copies, waits for them, and re-layouts: 124 us -> 28.5 us
  other arithmetic: 61.5 us -> 14.1 us
    pallas_call x0 -> x2, Pallas kernels: none -> 220 us  [the longest x1 160 us: exchange(): pl.pallas_call(functools.partial(gather_kernel, zs, xs, ys, halves), out_...]
    psum x4 -> x0, waiting for transfers between devices: 149 us -> none  [the longest x1 90.5 us: broadcast(): return lax.psum(block, axis)]
    all_gather x1, waiting for transfers between devices: 175 us -> 53.4 us  [body(): lax.all_gather(jnp.concatenate([piv_part, slot_row], axis=0), ('row', 'co...]
    dot_general x16 -> x26, matrix products: 178 us -> 77.9 us  [the longest x11 45.1 us: dot(): lax.dot_general(a, b, (((ca,), (cb,)), ((), ())), precision=lax.Precision...]
    gather x7 -> x0, local copies, waits for them, and re-layouts: 57.4 us -> none  [the longest x2 29.1 us: body(): every_panel = jnp.take(gathered, piv_owner * per_owner + piv_rank, axis=1)]
    select_n x11 -> x10, other arithmetic: 26.9 us -> 3.65 us  [the longest x3 2.14 us: pair_scale(): down = jnp.where(slot == 0, 0.0, jnp.roll(coupled, 1))]
    add x7 -> x6, other arithmetic: 20.5 us -> 0.88 us  [the longest x2 0.86 us: pair_scale(): return scaled * diag_part + nxt * up + prv * down]
    add x1 -> x0, local copies, waits for them, and re-layouts: 18.7 us -> none  [body(): front + lax.dot_general(flat_vals, col_hit, (((0,), (0,)), ((), ())), pre...]
  transfers between devices with their start and end apart: 7 -> 2, of which waited for: 6 -> 1; matrix products, arithmetic and copies ran while one was open for 11% -> 7% of each run, Pallas kernels for 0% -> 0%
where the time goes in v1:
time: 423 us; the launch traced here: 415 us
  Pallas kernels  220 us (52%)
  matrix products  77.9 us (18%)
  waiting for transfers between devices  53.4 us (13%)
  local copies, waits for them, and re-layouts  28.5 us (7%)
  between operations  15 us (4%)
  other arithmetic  14.1 us (3%)
  starting transfers between devices  5.71 us (1%)
    pallas_call x1, Pallas kernels, exchange(): pl.pallas_call(functools.partial(gather_kernel, zs, xs, ys, halves), out_...  160 us
    pallas_call x1, Pallas kernels, update(): pl.pallas_call(functools.partial(trailing_kernel, tile), grid=(rows // ti...  59.8 us
    all_gather x1, waiting for transfers between devices, body(): lax.all_gather(jnp.concatenate([piv_part, slot_row], axis=0), ('row', 'co...  53.4 us
    dot_general x11, matrix products, dot(): lax.dot_general(a, b, (((ca,), (cb,)), ((), ())), precision=lax.Precision...  45.1 us
    dot_general x15, matrix products, pick(): lax.dot_general(ones.astype(jnp.bfloat16), part.astype(jnp.bfloat16), (((...  32.8 us
  transfers between devices with their start and end apart: 2, of which 1 were waited for; matrix products, arithmetic and copies ran while one was open for 7% of the time, Pallas kernels for 0%

profile of v1, /device:TPU:5, one launch (start us, length us, event | category | flops | bytes accessed | tf_op | source)
XLA Modules:
  0.0 414.5 jit_solution(4496381067001617687)
XLA Ops:
  7.2 0.7 subtract_select_fusion.1
  7.9 2.3 convert_reduce_fusion
  10.5 9.6 %fusion.2 = f32[128,3072]{1,0:T(8,128)S(1)} fusion(f32[3072,1536]{1,0:T(8,128)} %front_ref.1, s32[128]{0:T(128)S(1)} %select_reduce_fusion.1), kind=kOutput, calls=%fused_computation.7 | convolution fusion | flops 1217986560 | bytes 20447744 | tf_op jit(solution)/shard_map/dot_general | solution.py:23
  20.1 8.1 %fusion.15 = f32[128,3072]{1,0:T(8,128)S(1)} fusion(f32[128,3072]{1,0:T(8,128)S(1)} %fusion.2, f32[3072,1536]{1,0:T(8,128)} %front_ref.1, s32[128]{0:T(128)S(1)} %select_reduce_fusion.1), kind=kOutput, calls=%fused_computation.23 | convolution fusion | flops 1227816960 | bytes 22020608 | tf_op jit(solution)/shard_map/dot_general | solution.py:23
  28.2 8.4 %fusion.12 = f32[128,3072]{1,0:T(8,128)S(1)} fusion(f32[128,3072]{1,0:T(8,128)S(1)} %fusion.15, f32[3072,1536]{1,0:T(8,128)} %front_ref.1, s32[128]{0:T(128)S(1)} %select_reduce_fusion.1), kind=kOutput, calls=%fused_computation.22 | convolution fusion | flops 1237254144 | bytes 22020608 | tf_op jit(solution)/shard_map/dot_general | solution.py:23
  36.9 0.7 fusion.17
  37.7 0.8 fusion.16
  38.5 0.7 fusion.47
  39.2 0.7 select_maximum_fusion
  39.9 1.3 pad_maximum_fusion
  41.2 2.2 reshape.232
  43.5 2.5 copy.22
  46.0 4.1 reshape.233
  50.1 5.7 %all-to-all-start = ((f32[8,136,384]{2,1,0:T(8,128)}), f32[8,136,384]{2,1,0:T(8,128)S(1)}, u32[]{:S(2)}, u32[]{:S(2)}) async-start(f32[8,136,384]{2,1,0:T(8,128)} %reshape.233), calls=%async_computation | async-start | bytes 3342336 | tf_op jit(solution)/shard_map/all_to_all | solution.py:334
  55.9 1.0 compare_reduce_fusion.1
  56.9 2.0 compare_reduce_fusion
  62.1 1.7 copy.19.rkeep_ref
  63.7 0.7 compare_select_fusion
  64.4 0.6 stack.16.coef_ref
  65.1 0.7 maximum_select_fusion
  65.8 0.7 maximum_select_fusion.1
  66.5 0.7 maximum_select_fusion.2
  67.2 1.7 convert_convert_fusion
  68.9 53.4 %all-gather.3.cloned.1.call-done = f32[4608,256]{1,0:T(8,128)} async-done(((f32[144,256]{1,0:T(8,128)}), f32[4608,256]{1,0:T(8,128)}) %all-gather.3.cloned.1.call-update) | async-done | bytes 4718608 | tf_op jit(solution)/shard_map/all_gather | solution.py:328
  122.3 0.8 slice.253
  123.2 2.7 fusion.101
  125.9 1.1 constant_dynamic-update-slice_fusion.4
  127.0 1.1 constant_dynamic-update-slice_fusion.3
  128.0 1.1 constant_dynamic-update-slice_fusion.2
  129.1 1.1 constant_dynamic-update-slice_fusion.1
  130.2 1.3 constant_dynamic-update-slice_fusion
  131.4 24.1 %fusion.7 = f32[1408,1024]{1,0:T(8,128)S(1)} fusion(f32[1088,1408]{1,0:T(8,128)} %constant_dynamic-update-slice_fusion, s32[1088]{0:T(1024)S(1)} %eq.233, s32[1024]{0:T(1024)S(1)} %multiply_add_fusion.1, s32[1088]{0:T(1024)S(1)} %select_n.160), kind=kOutput, calls=%fused_computation.13 | convolution fusion | flops 18827378688 | bytes 11907584 | tf_op jit(solution)/shard_map/dot_general | solution.py:15
  155.6 1.5 fusion.27
  157.3 2.2 copy-done.3
  160.2 0.6 convolution_add_fusion.1
  160.8 0.6 convolution_add_fusion
  161.9 2.5 fusion.78
  164.5 2.5 convolution_subtract_fusion.1
  167.0 2.8 convolution_subtract_fusion.2
  169.8 1.5 fusion.86
  173.4 2.5 fusion.76
  175.9 2.5 convolution_subtract_fusion
  178.5 1.5 fusion.84
  181.3 3.0 fusion.35
  184.4 0.7 fusion.71
  185.7 1.6 copy.18
  187.3 160.1 %shard_map.95 = (f32[2,8,192,1024]{3,2,1,0:T(8,128)}, f32[8,192,1024]{2,1,0:T(8,128)}) custom-call(f32[2,192,1024]{2,1,0:T(8,128)} %bitcast.51), custom_call_target="tpu_custom_call" | custom-call | tf_op jit(solution)/shard_map/pallas_call | solution.py:201
  347.4 59.8 %shard_map.96 = (f32[3072,1536]{1,0:T(8,128)}, f32[3072,1024]{1,0:T(8,128)}) custom-call(f32[3072,1024]{1,0:T(8,128)} %bitcast.47, f32[1536,1024]{1,0:T(8,128)} %bitcast.50, f32[3072,1536]{1,0:T(8,128)} %front_ref.1, f32[3072,1]{1,0:T(8,128)} %copy.19.rkeep_ref, f32[1,1536]{1,0:T(1,128)} %select_n.171.ckeep_ref, f32[8,1024]{1,0:T(8,128)} %stack.16.coef_ref), custom_call_target="tpu_custom_call" | custom-call | tf_op jit(solution)/shard_map/pallas_call | solution.py:263
  (75 shorter events, 9.2 us)
Async XLA Ops:
  7.2 115.2 %all-gather.3.cloned.1.call-start = ((), (), s32[]{:S(2)}) async-start(), calls=%async_computation.1 | async-start | bytes 4866048 | tf_op jit(solution)/shard_map/all_gather | solution.py:328
  28.2 8.7 %copy-start.6 = (f32[8,3072]{1,0:T(8,128)S(1)}, f32[8,3072]{1,0:T(8,128)}, u32[]{:S(2)}) copy-start(f32[8,3072]{1,0:T(8,128)} %param.9) | copy-start | bytes 294916
  37.7 0.8 copy-start.11
  50.1 5.7 %copy-start.7 = (s32[1024]{0:T(1024)S(1)}, s32[1024]{0:T(1024)}, u32[]{:S(2)}) copy-start(s32[1024]{0:T(1024)} %param.11) | copy-start | bytes 12292
  50.1 8.7 %copy-start.9 = (f32[1024]{0:T(1024)S(1)}, f32[1024]{0:T(1024)}, u32[]{:S(2)}) copy-start(f32[1024]{0:T(1024)} %param.15) | copy-start | bytes 12292
  50.1 8.8 %copy-start.10 = (s32[1024]{0:T(1024)S(1)}, s32[1024]{0:T(1024)}, u32[]{:S(2)}) copy-start(s32[1024]{0:T(1024)} %param.12) | copy-start | bytes 12292
  50.1 8.8 %copy-start.8 = (f32[1024]{0:T(1024)S(1)}, f32[1024]{0:T(1024)}, u32[]{:S(2)}) copy-start(f32[1024]{0:T(1024)} %param.14) | copy-start | bytes 12292
  50.1 80.0 %all-to-all-start = ((f32[8,136,384]{2,1,0:T(8,128)}), f32[8,136,384]{2,1,0:T(8,128)S(1)}, u32[]{:S(2)}, u32[]{:S(2)}) async-start(f32[8,136,384]{2,1,0:T(8,128)} %reshape.233), calls=%async_computation | async-start | bytes 3342336 | tf_op jit(solution)/shard_map/all_to_all | solution.py:334
  131.4 24.1 %copy-start.5 = (f32[4,256,256]{2,1,0:T(8,128)S(1)}, f32[4,256,256]{2,1,0:T(8,128)}, u32[]{:S(2)}) copy-start(f32[4,256,256]{2,1,0:T(8,128)} %param.13) | copy-start | bytes 3145732
  155.5 11.4 %copy-start.4 = (f32[1408,1024]{1,0:T(8,128)}, f32[1408,1024]{1,0:T(8,128)S(1)}, u32[]{:S(2)}) copy-start(f32[1408,1024]{1,0:T(8,128)S(1)} %fusion.7) | copy-start | bytes 17301508
  157.1 4.4 %copy-start.2 = (f32[1408,256]{0,1:T(8,128)}, f32[1408,256]{0,1:T(8,128)S(1)}, u32[]{:S(2)}) copy-start(f32[1408,256]{0,1:T(8,128)S(1)} %fusion.27) | copy-start | bytes 4325380
  157.1 2.5 copy-start.3
  171.3 1.7 copy-start.1
  180.0 1.3 copy-start
  181.3 3.0 slice-start.3
  184.3 1.0 slice-start
  184.4 1.1 slice-start.1
  184.4 1.2 slice-start.2
Sparse Core Ops, SparseCore 0:
  40.1 82.2 all-gather.2
